TPU v7x, 32 devices: a whole 2x2x4 slice. The times are simulated.
32 devices in a mesh: expert: 8 (over z, x), dp: 4 (over y, core).
Axes of the slice: x: 2, y: 2, z: 4, core: 2. Of those that a mesh axis runs over, the one named last changes fastest.
Arguments:
- features: bfloat16 [4096, 32, 64], P(('expert', 'dp')), may hold values from -1 to 1
- spacing: float32 [4096, 32], P(('expert', 'dp')), may hold values from 0.02 to 0.3
- targets: float32 [3, 4096], P(None, ('expert', 'dp')), may hold values from 0 to 1
- ray_length: int32 [4096], P(('expert', 'dp')), may hold values from 1 to 32, as said below
- cell_id: int32 [4096, 32], P(('expert', 'dp')), may hold values from 0 to 15, as said below
- slot_rank: int32 [4096, 32], P(('expert', 'dp')), may hold values from -1 to 383, as said below
- image_id: int32 [4096], P(('expert', 'dp')), may hold values from 0 to 511, as said below
- params: float32 [16, 848, 256], P('expert'), may hold values from -5 to 5
- first_moment: float32 [16, 848, 256], P('expert'), may hold values from -0.75 to 0.75
- second_moment: float32 [16, 848, 256], P('expert'), may hold values from 1e-06 to 0.01
- code_table: float32 [512, 64], P(('expert', 'dp')), may hold values from -6 to 6
- table_first: float32 [512, 64], P(('expert', 'dp')), may hold values from -0.75 to 0.75
- table_second: float32 [512, 64], P(('expert', 'dp')), may hold values from 1e-06 to 0.01
Outputs:
- ray_loss: float32 [4096], P(('expert', 'dp'))
- new_params: float32 [16, 848, 256], P('expert')
- new_first_moment: float32 [16, 848, 256], P('expert')
- new_second_moment: float32 [16, 848, 256], P('expert')
- new_code_table: float32 [512, 64], P(('expert', 'dp'))
- new_table_first: float32 [512, 64], P(('expert', 'dp'))
- new_table_second: float32 [512, 64], P(('expert', 'dp'))
Inputs may be any that keep to these rules, and one draw needn't show every extreme that they name: `ray_length`: rays form aligned blocks of 128, one a device, in the order of the axes expert then dp. In every block the lengths sum to 3072 and some ray has all 32 samples. `cell_id`: also given for samples at or beyond their ray's length, where it is unused. `slot_rank`: for a sample below its ray's length: its rank among the live samples of its block of 128 rays that have the same cell_id, counted ray by ray and along each ray; -1 for the other samples. No block has more than 384 live samples of one cell_id; in every block some cell_id has exactly 384, and one cell_id has 384 in every block. `image_id`: A ray of block b names an image from b * 16 to (b + 1) * 16 - 1.
All inputs are finite; a program needn't handle non-finite values.
Results may differ from a plain program's by a relative error of at most 0.0046.
Values may be sent and summed in bfloat16 or wider, within the bound.
A program may use at most 128 MiB of HBM per device.

v0:
```python
import jax
import jax.numpy as jnp
from jax import lax
from jax.sharding import PartitionSpec as P

NET_WIDTH = 256
CODE_WIDTH = 64
ENC_WIDTH = 64
LAYERS = 4
SAMPLES = 32
BETA_ONE = 0.9
BETA_TWO = 0.999
LEARN_RATE = 0.001
ADAM_EPS = 1e-08
CORRECT_ONE = 1.0 - 0.9**10
CORRECT_TWO = 1.0 - 0.999**10


def adam_update(param_now, gradient, moment_one, moment_two):
    new_one = BETA_ONE * moment_one + (1.0 - BETA_ONE) * gradient
    new_two = BETA_TWO * moment_two + (1.0 - BETA_TWO) * gradient * gradient
    update = LEARN_RATE * (new_one / CORRECT_ONE) / (jnp.sqrt(new_two / CORRECT_TWO) + ADAM_EPS)
    return (param_now - update, new_one, new_two)


def composite(raw_out, spacing, live_mask, targets):
    density = jax.nn.softplus(raw_out[0])
    colors = jax.nn.sigmoid(raw_out[1:4])
    optical = density * spacing * live_mask
    before = jnp.cumsum(optical, axis=1) - optical
    weight = jnp.exp(-before) * (1.0 - jnp.exp(-optical))
    render = jnp.sum(weight[None] * colors, axis=2)
    return 0.5 * jnp.sum((render - targets) ** 2, axis=0)


def place_rows(rows, slot_index, slots_all):
    blank = jnp.zeros((slots_all,) + rows.shape[1:], rows.dtype)
    return blank.at[slot_index].set(rows, mode="drop")


def pick_rows(buffer, slot_index):
    return jnp.take(buffer, slot_index, axis=0, mode="fill", fill_value=0)


def hidden_pass(weights_bf, inputs):
    head_row = ENC_WIDTH + (LAYERS - 1) * NET_WIDTH
    activations = [inputs]
    preacts = []
    current = inputs
    row_start = 0
    row_count = ENC_WIDTH
    for layer_index in range(LAYERS):
        matrix = weights_bf[:, row_start : row_start + row_count, :]
        bias_row = weights_bf[:, head_row + 9 + layer_index, :].astype(jnp.float32)
        preact = (
            jnp.einsum("enr,erw->enw", current, matrix, preferred_element_type=jnp.float32)
            + bias_row[:, None, :]
        )
        current = jnp.maximum(preact, 0.0).astype(jnp.bfloat16)
        preacts.append(preact)
        activations.append(current)
        row_start = row_start + row_count
        row_count = NET_WIDTH
    return (activations, preacts)


def hidden_grads(weights_bf, activations, preacts, upstream):
    weight_grads = [None] * LAYERS
    bias_grads = [None] * LAYERS
    for layer_index in reversed(range(LAYERS)):
        pre_grad = jnp.where(preacts[layer_index] > 0, upstream, 0.0).astype(jnp.bfloat16)
        weight_grads[layer_index] = jnp.einsum(
            "enr,enw->erw", activations[layer_index], pre_grad, preferred_element_type=jnp.float32
        )
        bias_grads[layer_index] = jnp.sum(pre_grad, axis=1, dtype=jnp.float32)
        if layer_index > 0:
            row_start = ENC_WIDTH + (layer_index - 1) * NET_WIDTH
            upstream = jnp.einsum(
                "enw,erw->enr",
                pre_grad,
                weights_bf[:, row_start : row_start + NET_WIDTH, :],
                preferred_element_type=jnp.float32,
            )
    return (weight_grads, bias_grads)


def assemble(weight_grads, bias_grads, hidden_grad, code_grad_head, bias_grad_head):
    held_count = hidden_grad.shape[0]
    pieces = list(weight_grads) + [
        hidden_grad,
        jnp.pad(code_grad_head, ((0, 0), (0, 0), (0, NET_WIDTH - CODE_WIDTH))),
        jnp.pad(bias_grad_head, ((0, 0), (0, NET_WIDTH - 4)))[:, None, :],
        jnp.stack(bias_grads, axis=1),
        jnp.zeros((held_count, 7 - LAYERS, NET_WIDTH), jnp.float32),
    ]
    return jnp.concatenate(pieces, axis=1)


def shards(
    features,
    spacing,
    targets,
    ray_length,
    cell_id,
    slot_rank,
    image_id,
    params,
    first_moment,
    second_moment,
    code_table,
    table_first,
    table_second,
):
    ray_rows = features.shape[0]
    sample_count = ray_rows * SAMPLES
    groups = lax.axis_size("expert")
    held_count = params.shape[0]
    experts_all = held_count * groups
    capacity = 2 * (sample_count * 3 // 4 // experts_all)
    slots_all = experts_all * capacity
    head_row = ENC_WIDTH + (LAYERS - 1) * NET_WIDTH
    weights_bf = params.astype(jnp.bfloat16)
    table_rows = code_table.shape[0]
    block_index = lax.axis_index("expert") * lax.axis_size("dp") + lax.axis_index("dp")
    local_image = image_id - block_index * table_rows
    picker = (local_image[:, None] == jnp.arange(table_rows, dtype=jnp.int32)[None, :]).astype(
        jnp.bfloat16
    )
    ray_code = jnp.dot(
        picker, code_table.astype(jnp.bfloat16), preferred_element_type=jnp.float32
    ).astype(jnp.bfloat16)
    position = jnp.arange(SAMPLES, dtype=jnp.int32)
    live_mask = (position[None, :] < ray_length[:, None]).astype(jnp.float32)
    flat_rank = slot_rank.reshape(sample_count)
    slot_index = jnp.where(
        flat_rank >= 0, cell_id.reshape(sample_count) * capacity + flat_rank, slots_all
    )
    positions = features.reshape(sample_count, ENC_WIDTH)
    sample_code = jnp.broadcast_to(ray_code[:, None, :], (ray_rows, SAMPLES, CODE_WIDTH)).reshape(
        sample_count, CODE_WIDTH
    )
    outgoing = place_rows(
        jnp.concatenate([positions, sample_code], axis=1), slot_index, slots_all
    ).reshape(experts_all, capacity, ENC_WIDTH + CODE_WIDTH)
    arrived = lax.all_to_all(outgoing, "expert", split_axis=0, concat_axis=1, tiled=True)
    hidden_head = weights_bf[:, head_row : head_row + 4, :]
    inputs = arrived[:, :, :ENC_WIDTH]
    code_rows = arrived[:, :, ENC_WIDTH:]
    activations, preacts = hidden_pass(weights_bf, inputs)
    raw_out = jnp.einsum(
        "enw,ecw->enc", activations[-1], hidden_head, preferred_element_type=jnp.float32
    )
    code_head = weights_bf[:, head_row + 4 : head_row + 8, :CODE_WIDTH]
    raw_out = raw_out + jnp.einsum(
        "enk,eck->enc", code_rows, code_head, preferred_element_type=jnp.float32
    )
    raw_out = raw_out + weights_bf[:, head_row + 8, :4].astype(jnp.float32)[:, None, :]
    returned = lax.all_to_all(raw_out, "expert", split_axis=1, concat_axis=0, tiled=True)
    raw_samples = pick_rows(returned.reshape(slots_all, 4), slot_index)
    raw_grid = raw_samples.T.reshape(4, ray_rows, SAMPLES)

    def loss_of(raw_in):
        return composite(raw_in, spacing, live_mask, targets)

    ray_loss, pullback = jax.vjp(loss_of, raw_grid)
    (raw_grad,) = pullback(jnp.ones_like(ray_loss))
    cotangent = raw_grad.reshape(4, sample_count).T.astype(jnp.bfloat16)
    cot_slots = place_rows(cotangent, slot_index, slots_all).reshape(experts_all, capacity, 4)
    cot_in = lax.all_to_all(cot_slots, "expert", split_axis=0, concat_axis=1, tiled=True)
    upstream = jnp.einsum("enc,ecw->enw", cot_in, hidden_head, preferred_element_type=jnp.float32)
    weight_grads, bias_grads = hidden_grads(weights_bf, activations, preacts, upstream)
    hidden_grad = jnp.einsum(
        "enc,enw->ecw", cot_in, activations[-1], preferred_element_type=jnp.float32
    )
    code_grad_head = jnp.einsum(
        "enc,enk->eck", cot_in, code_rows, preferred_element_type=jnp.float32
    )
    bias_grad_head = jnp.sum(cot_in, axis=1, dtype=jnp.float32)
    code_back = jnp.einsum("enc,eck->enk", cot_in, code_head, preferred_element_type=jnp.float32)
    code_back = code_back.reshape(held_count, groups * capacity // 2, 2 * CODE_WIDTH)
    code_slot_grad = lax.all_to_all(
        code_back, "expert", split_axis=1, concat_axis=0, tiled=True
    ).reshape(slots_all, CODE_WIDTH)
    local_grad = assemble(weight_grads, bias_grads, hidden_grad, code_grad_head, bias_grad_head)
    param_grad = lax.psum(local_grad, "dp")
    sample_code_grad = pick_rows(code_slot_grad, slot_index).reshape(ray_rows, SAMPLES, CODE_WIDTH)
    ray_code_grad = jnp.sum(sample_code_grad, axis=1)
    table_grad = lax.dot_general(
        picker.astype(jnp.float32),
        ray_code_grad,
        (((0,), (0,)), ((), ())),
        precision=lax.Precision.HIGHEST,
        preferred_element_type=jnp.float32,
    )
    new_params, new_first, new_second = adam_update(params, param_grad, first_moment, second_moment)
    new_table, new_table_first, new_table_second = adam_update(
        code_table, table_grad, table_first, table_second
    )
    return (
        ray_loss,
        new_params,
        new_first,
        new_second,
        new_table,
        new_table_first,
        new_table_second,
    )


def solution(mesh):
    return jax.shard_map(
        shards,
        mesh=mesh,
        in_specs=(
            P(("expert", "dp"), None, None),
            P(("expert", "dp"), None),
            P(None, ("expert", "dp")),
            P(("expert", "dp")),
            P(("expert", "dp"), None),
            P(("expert", "dp"), None),
            P(("expert", "dp")),
            P("expert", None, None),
            P("expert", None, None),
            P("expert", None, None),
            P(("expert", "dp"), None),
            P(("expert", "dp"), None),
            P(("expert", "dp"), None),
        ),
        out_specs=(
            P(("expert", "dp")),
            P("expert", None, None),
            P("expert", None, None),
            P("expert", None, None),
            P(("expert", "dp"), None),
            P(("expert", "dp"), None),
            P(("expert", "dp"), None),
        ),
        check_vma=False,
    )
```

profile of v0, /device:TPU:0, one launch (start us, length us, event | category | flops | bytes accessed | tf_op | source)
XLA Modules:
  0.0 286.6 jit_solution(14919669906394410517)
XLA Ops:
  13.4 13.5 %scatter_custom_fusion = bf16[6144,128]{1,0:T(8,128)(2,1)} fusion(s32[4096]{0:T(1024)S(1)} %bitcast.80, bf16[4096,64]{1,0:T(8,128)(2,1)} %bitcast.72, bf16[]{:T(256)} %constant.118, bf16[4096,64]{1,0:T(8,128)(2,1)S(1)} %bitcast.71, bf16[]{:T(256)} %constant.35.clone.1), kind=kCustom, calls=%fused_computation.37 | custom fusion | flops 2097152 | bytes 3145732 | tf_op jit(solution)/shard_map/scatter | solution.py:38
  26.9 7.6 %all-to-all-start = ((bf16[16,384,128]{2,1,0:T(8,128)(2,1)}), bf16[16,384,128]{2,1,0:T(8,128)(2,1)S(1)}, u32[]{:S(2)}, u32[]{:S(2)}) async-start(bf16[16,384,128]{2,1,0:T(8,128)(2,1)} %bitcast.68), calls=%async_computation | async-start | bytes 3145728 | tf_op jit(solution)/shard_map/all_to_all | solution.py:145
  35.6 35.9 %all-to-all-done = bf16[16,384,128]{2,1,0:T(8,128)(2,1)S(1)} async-done(((bf16[16,384,128]{2,1,0:T(8,128)(2,1)}), bf16[16,384,128]{2,1,0:T(8,128)(2,1)S(1)}, u32[]{:S(2)}, u32[]{:S(2)}) %all-to-all-start) | async-done | bytes 1572896 | tf_op jit(solution)/shard_map/all_to_all | solution.py:145
  73.4 4.1 %fusion.2 = (u8[3072,256]{1,0:T(8,128)(4,1)}, f32[2,3072,256]{2,1,0:T(8,128)S(1)}) fusion(f32[2,256]{1,0:T(2,128)S(1)} %bitcast.86, bf16[2,848,256]{2,1,0:T(8,128)(2,1)} %copy-done.9, bf16[2,3072,128]{1,2,0:T(8,128)(2,1)S(1)} %all_to_all.51), kind=kOutput, calls=%fused_computation.32 | convolution fusion | flops 209977344 | bytes 7931904 | tf_op jit(solution)/shard_map/enr,erw->enw/dot_general | solution.py:56
  77.5 3.1 %fusion.3 = (u8[3072,256]{1,0:T(8,128)(4,1)}, f32[2,3072,256]{2,1,0:T(8,128)S(1)}) fusion(f32[2,256]{1,0:T(2,128)S(1)} %get-tuple-element.38, bf16[2,848,256]{2,1,0:T(8,128)(2,1)S(1)} %copy-done.10, f32[2,3072,256]{2,1,0:T(8,128)S(1)} %get-tuple-element.28, f32[2,256]{1,0:T(2,128)S(1)} %bitcast.87), kind=kOutput, calls=%fused_computation.33 | convolution fusion | flops 818675712 | bytes 13635584 | tf_op jit(solution)/shard_map/enr,erw->enw/dot_general | solution.py:56
  80.6 3.1 %fusion.4 = (u8[3072,256]{1,0:T(8,128)(4,1)}, f32[2,3072,256]{2,1,0:T(8,128)S(1)}) fusion(f32[2,256]{1,0:T(2,128)S(1)} %get-tuple-element.37, bf16[2,848,256]{2,1,0:T(8,128)(2,1)S(1)} %copy-done.10, f32[2,3072,256]{2,1,0:T(8,128)S(1)} %get-tuple-element.26, f32[2,256]{1,0:T(2,128)S(1)} %get-tuple-element.38), kind=kOutput, calls=%fused_computation.34 | convolution fusion | flops 818675712 | bytes 13635584 | tf_op jit(solution)/shard_map/enr,erw->enw/dot_general | solution.py:56
  83.7 3.1 %fusion.5 = (u8[3072,256]{1,0:T(8,128)(4,1)}, f32[2,3072,256]{2,1,0:T(8,128)S(1)}) fusion(f32[2,256]{1,0:T(2,128)S(1)} %bitcast.83, bf16[2,848,256]{2,1,0:T(8,128)(2,1)S(1)} %copy-done.10, f32[2,3072,256]{2,1,0:T(8,128)S(1)} %get-tuple-element.24, f32[2,256]{1,0:T(2,128)S(1)} %get-tuple-element.37), kind=kOutput, calls=%fused_computation.35 | convolution fusion | flops 818675712 | bytes 13635584 | tf_op jit(solution)/shard_map/enr,erw->enw/dot_general | solution.py:56
  89.7 2.9 %copy.96 = f32[2,3072,4]{2,0,1:T(2,128)S(1)} copy(f32[2,3072,4]{1,2,0:T(4,128)S(1)} %fusion) | data formatting | bytes 196608 | tf_op jit(solution)/shard_map/add | solution.py:157
  92.6 5.6 %reshape.184 = f32[8,1,3072]{2,1,0:T(1,128)} reshape(f32[3072,2,4]{2,1,0:T(2,128)S(1)} %bitcast.65) | data formatting | bytes 196608
  98.2 4.2 %all-to-all-start.1 = ((f32[8,1,3072]{2,1,0:T(1,128)}), f32[8,1,3072]{2,1,0:T(1,128)S(1)}, u32[]{:S(2)}, u32[]{:S(2)}) async-start(f32[8,1,3072]{2,1,0:T(1,128)} %reshape.184), calls=%async_computation.1 | async-start | bytes 196608 | tf_op jit(solution)/shard_map/all_to_all | solution.py:158
  102.4 7.1 %all-to-all-done.1 = f32[8,1,3072]{2,1,0:T(1,128)S(1)} async-done(((f32[8,1,3072]{2,1,0:T(1,128)}), f32[8,1,3072]{2,1,0:T(1,128)S(1)}, u32[]{:S(2)}, u32[]{:S(2)}) %all-to-all-start.1) | async-done | bytes 98336 | tf_op jit(solution)/shard_map/all_to_all | solution.py:158
  110.9 6.6 %reshape.185 = f32[3072,2,4]{2,1,0:T(2,128)} reshape(f32[8,3072]{1,0:T(8,128)S(1)} %reduce.14) | data formatting | bytes 196608
  119.7 14.1 %gather_fusion = f32[4096,4]{1,0:T(8,128)} fusion(f32[6144,4]{1,0:T(8,128)S(1)} %bitcast.60, s32[4096]{0:T(1024)S(1)} %broadcast_clamp_fusion), kind=kCustom, calls=%fused_computation | custom fusion | bytes 147456 | tf_op jit(solution)/shard_map/jit(_take)/gather | solution.py:42
  138.3 11.4 %scatter_custom_fusion.1 = bf16[6144,4]{1,0:T(8,128)(2,1)S(1)} fusion(s32[4096]{0:T(1024)S(1)} %bitcast.82, bf16[4096,4]{1,0:T(8,128)(2,1)S(1)} %copy.113, bf16[]{:T(256)} %constant.35.clone.1), kind=kCustom, calls=%fused_computation.49 | custom fusion | bytes 49154 | tf_op jit(solution)/shard_map/scatter | solution.py:38
  150.4 9.3 %all_to_all.66 = bf16[16,384,4]{1,2,0:T(4,128)(2,1)S(1)} all-to-all(bf16[16,384,4]{1,2,0:T(4,128)(2,1)S(1)} %copy.114), channel_id=1, replica_groups=mesh['expert'=8,'dp'=4] {'expert'}, dimensions={0} | all-to-all | bytes 98304 | tf_op jit(solution)/shard_map/all_to_all | solution.py:169
  159.8 3.6 %fusion.16 = f32[2,4,256]{2,1,0:T(4,128)S(1)} fusion(bf16[2,3072,4]{1,2,0:T(4,128)(2,1)S(1)} %bitcast.73, f32[2,3072,256]{2,1,0:T(8,128)} %copy-done.3, f32[2,256]{1,0:T(2,128)S(1)} %bitcast.85), kind=kOutput, calls=%fused_computation.47 | convolution fusion | flops 17301504 | bytes 6350848 | tf_op jit(solution)/shard_map/enc,enw->ecw/dot_general | solution.py:172
  172.2 3.0 %convert_reduce_fusion.3 = (f32[2,256]{1,0:T(2,128)S(1)}, bf16[2,3072,256]{2,1,0:T(8,128)(2,1)}) fusion(bf16[2,3072,256]{2,1,0:T(8,128)(2,1)S(1)} %get-tuple-element.32, bf16[2,848,256]{2,1,0:T(8,128)(2,1)S(1)} %copy-done.11, u8[3072,256]{1,0:T(8,128)(4,1)S(1)} %copy-done.16), kind=kOutput, calls=%fused_computation.16 | convolution fusion | flops 817888768 | bytes 7342080 | tf_op jit(solution)/shard_map/enw,erw->enr/dot_general | solution.py:78
  176.7 7.0 %copy.121 = f32[2,1536,128]{2,0,1:T(2,128)} copy(f32[2,1536,128]{2,1,0:T(8,128)} %reshape.134) | data formatting | bytes 3145728 | tf_op jit(solution)/shard_map/reshape | solution.py:180
  183.7 3.6 %all-to-all-start.3 = ((f32[2,1536,128]{2,0,1:T(2,128)}), f32[2,1536,128]{2,0,1:T(2,128)S(1)}, u32[]{:S(2)}, u32[]{:S(2)}) async-start(f32[2,1536,128]{2,0,1:T(2,128)} %copy.121), calls=%async_computation.3 | async-start | bytes 3145728 | tf_op jit(solution)/shard_map/all_to_all | solution.py:181
  190.4 5.4 %fusion.12 = f32[2,256,256]{2,1,0:T(8,128)} fusion(bf16[2,3072,256]{2,1,0:T(8,128)(2,1)S(1)} %copy-done.13, f32[2,3072,256]{2,1,0:T(8,128)} %copy-done.1, f32[2,256]{1,0:T(2,128)S(1)} %get-tuple-element.38), kind=kOutput, calls=%fused_computation.43 | convolution fusion | flops 810024960 | bytes 9963520 | tf_op jit(solution)/shard_map/enr,enw->erw/dot_general | solution.py:72
  198.1 7.2 %concatenate.7 = f32[2,848,256]{2,1,0:T(8,128)} concatenate(f32[2,64,256]{2,1,0:T(8,128)S(1)} %fusion.24, f32[2,256,256]{2,1,0:T(8,128)} %fusion.10, f32[2,256,256]{2,1,0:T(8,128)} %fusion.12, f32[2,256,256]{2,1,0:T(8,128)} %fusion.14, f32[2,4,256]{2,1,0:T(4,128)S(1)} %fusion.16, f32[2,4,256]{2,1,0:T(4,128)S(1)} %pad.16, f32[2,1,256]{2,1,0:T(1,128)S(1)} %broadcast_in_dim.84, ...), dimensions={1} | concatenate | bytes 3473408 | tf_op jit(solution)/shard_map/concatenate | solution.py:96
  206.0 46.4 %all-reduce.6.cloned.1.call-done = f32[2,848,256]{2,1,0:T(8,128)} async-done(((f32[2,848,256]{2,1,0:T(8,128)}), f32[2,848,256]{2,1,0:T(8,128)}) %all-reduce.6.cloned.1.call-update) | async-done | bytes 1736720 | tf_op jit(solution)/shard_map/psum | solution.py:185
  252.4 5.5 %divide_subtract_fusion = (f32[2,848,256]{2,1,0:T(8,128)}, f32[2,848,256]{2,1,0:T(8,128)}, f32[2,848,256]{2,1,0:T(8,128)}) fusion(f32[2,848,256]{2,1,0:T(8,128)S(1)} %copy-done.5, f32[2,848,256]{2,1,0:T(8,128)} %all-reduce.6.cloned.1.call-done, f32[2,848,256]{2,1,0:T(8,128)} %param.21, f32[2,848,256]{2,1,0:T(8,128)} %param.22), kind=kLoop, calls=%fused_computation.30 | loop fusion | flops 5210112 | bytes 12156928 | tf_op jit(solution)/shard_map/sub | solution.py:23
  261.7 14.1 %gather_fusion.1 = f32[4096,64]{1,0:T(8,128)} fusion(f32[6144,64]{1,0:T(8,128)S(1)} %reshape.135, s32[4096]{0:T(1024)S(1)} %broadcast_clamp_fusion), kind=kCustom, calls=%fused_computation.1 | custom fusion | bytes 2113536 | tf_op jit(solution)/shard_map/jit(_take)/gather | solution.py:42
  (143 shorter events, 44.5 us)
Async XLA Ops:
  13.4 21.2 %copy-start.4 = (f32[2,848,256]{2,1,0:T(8,128)S(1)}, f32[2,848,256]{2,1,0:T(8,128)}, u32[]{:S(2)}) copy-start(f32[2,848,256]{2,1,0:T(8,128)} %param.20) | copy-start | bytes 5210116
  26.9 44.6 %all-to-all-start = ((bf16[16,384,128]{2,1,0:T(8,128)(2,1)}), bf16[16,384,128]{2,1,0:T(8,128)(2,1)S(1)}, u32[]{:S(2)}, u32[]{:S(2)}) async-start(bf16[16,384,128]{2,1,0:T(8,128)(2,1)} %bitcast.68), calls=%async_computation | async-start | bytes 3145728 | tf_op jit(solution)/shard_map/all_to_all | solution.py:145
  73.4 16.1 %copy-start.6 = (bf16[2,3072,128]{1,2,0:T(8,128)(2,1)}, bf16[2,3072,128]{1,2,0:T(8,128)(2,1)S(1)}, u32[]{:S(2)}) copy-start(bf16[2,3072,128]{1,2,0:T(8,128)(2,1)S(1)} %all_to_all.51) | copy-start | bytes 4718596
  73.4 4.1 %copy-start.10 = (bf16[2,848,256]{2,1,0:T(8,128)(2,1)S(1)}, bf16[2,848,256]{2,1,0:T(8,128)(2,1)}, u32[]{:S(2)}) copy-start(bf16[2,848,256]{2,1,0:T(8,128)(2,1)} %copy-done.9) | copy-start | bytes 2605060
  77.5 3.1 %copy-start = (f32[2,3072,256]{2,1,0:T(8,128)}, f32[2,3072,256]{2,1,0:T(8,128)S(1)}, u32[]{:S(2)}) copy-start(f32[2,3072,256]{2,1,0:T(8,128)S(1)} %get-tuple-element.28) | copy-start | bytes 18874372
  80.6 3.1 %copy-start.1 = (f32[2,3072,256]{2,1,0:T(8,128)}, f32[2,3072,256]{2,1,0:T(8,128)S(1)}, u32[]{:S(2)}) copy-start(f32[2,3072,256]{2,1,0:T(8,128)S(1)} %get-tuple-element.26) | copy-start | bytes 18874372
  83.7 3.1 %copy-start.2 = (f32[2,3072,256]{2,1,0:T(8,128)}, f32[2,3072,256]{2,1,0:T(8,128)S(1)}, u32[]{:S(2)}) copy-start(f32[2,3072,256]{2,1,0:T(8,128)S(1)} %get-tuple-element.24) | copy-start | bytes 18874372
  98.2 11.3 %all-to-all-start.1 = ((f32[8,1,3072]{2,1,0:T(1,128)}), f32[8,1,3072]{2,1,0:T(1,128)S(1)}, u32[]{:S(2)}, u32[]{:S(2)}) async-start(f32[8,1,3072]{2,1,0:T(1,128)} %reshape.184), calls=%async_computation.1 | async-start | bytes 196608 | tf_op jit(solution)/shard_map/all_to_all | solution.py:158
  119.7 16.6 %copy-start.20 = (f32[128,32]{0,1:T(8,128)S(1)}, f32[128,32]{0,1:T(8,128)}, u32[]{:S(2)}) copy-start(f32[128,32]{0,1:T(8,128)} %param.14) | copy-start | bytes 49156
  119.7 16.6 %copy-start.24 = (s32[128]{0:T(128)S(1)}, s32[128]{0:T(128)}, u32[]{:S(2)}) copy-start(s32[128]{0:T(128)} %param.16) | copy-start | bytes 1540
  133.8 2.9 %copy-start.25 = (f32[3,128]{1,0:T(4,128)S(1)}, f32[3,128]{1,0:T(4,128)}, u32[]{:S(2)}) copy-start(f32[3,128]{1,0:T(4,128)} %param.15) | copy-start | bytes 4612
  159.8 3.6 %copy-start.7 = (bf16[2,3072,128]{1,2,0:T(8,128)(2,1)S(1)}, bf16[2,3072,128]{1,2,0:T(8,128)(2,1)}, u32[]{:S(2)}) copy-start(bf16[2,3072,128]{1,2,0:T(8,128)(2,1)} %copy-done.6) | copy-start | bytes 4718596
  159.8 3.9 %copy-start.11 = (bf16[2,848,256]{2,1,0:T(8,128)(2,1)S(1)}, bf16[2,848,256]{2,1,0:T(8,128)(2,1)}, u32[]{:S(2)}) copy-start(bf16[2,848,256]{2,1,0:T(8,128)(2,1)} %copy-done.9) | copy-start | bytes 2605060
  172.1 3.1 %copy-start.14 = (bf16[2,3072,256]{2,1,0:T(8,128)(2,1)}, bf16[2,3072,256]{2,1,0:T(8,128)(2,1)S(1)}, u32[]{:S(2)}) copy-start(bf16[2,3072,256]{2,1,0:T(8,128)(2,1)S(1)} %get-tuple-element.32) | copy-start | bytes 9437188
  176.7 10.9 %copy-start.8 = (bf16[2,3072,128]{1,2,0:T(8,128)(2,1)S(1)}, bf16[2,3072,128]{1,2,0:T(8,128)(2,1)}, u32[]{:S(2)}) copy-start(bf16[2,3072,128]{1,2,0:T(8,128)(2,1)} %copy-done.6) | copy-start | bytes 4718596
  183.7 74.1 %all-to-all-start.3 = ((f32[2,1536,128]{2,0,1:T(2,128)}), f32[2,1536,128]{2,0,1:T(2,128)S(1)}, u32[]{:S(2)}, u32[]{:S(2)}) async-start(f32[2,1536,128]{2,0,1:T(2,128)} %copy.121), calls=%async_computation.3 | async-start | bytes 3145728 | tf_op jit(solution)/shard_map/all_to_all | solution.py:181
  187.3 65.0 %all-reduce.6.cloned.1.call-start = ((), (), s32[]{:S(2)}) async-start(), calls=%async_computation.4 | async-start | bytes 3473408 | tf_op jit(solution)/shard_map/psum | solution.py:185
  187.6 8.2 %slice-start = ((s8[6291456]{0:T(1024)(128)(4,1)}), s8[4194304]{0:T(1024)(128)(4,1)S(1)}, s32[]{:S(2)}) async-start(s8[6291456]{0:T(1024)(128)(4,1)} %bitcast.61), calls=%async_computation.5 | async-start | bytes 8388608
  190.4 5.4 %slice-start.1 = ((s8[6291456]{0:T(1024)(128)(4,1)}), s8[2097152]{0:T(1024)(128)(4,1)S(1)}, s32[]{:S(2)}) async-start(s8[6291456]{0:T(1024)(128)(4,1)} %bitcast.61), calls=%async_computation.6 | async-start | bytes 4194304
  190.4 5.4 %copy-start.15 = (bf16[2,3072,256]{2,1,0:T(8,128)(2,1)S(1)}, bf16[2,3072,256]{2,1,0:T(8,128)(2,1)}, u32[]{:S(2)}) copy-start(bf16[2,3072,256]{2,1,0:T(8,128)(2,1)} %copy-done.14) | copy-start | bytes 9437188
  198.1 54.2 %copy-start.5 = (f32[2,848,256]{2,1,0:T(8,128)S(1)}, f32[2,848,256]{2,1,0:T(8,128)}, u32[]{:S(2)}) copy-start(f32[2,848,256]{2,1,0:T(8,128)} %param.20) | copy-start | bytes 5210116
  261.6 17.0 %copy-start.21 = (f32[16,64]{1,0:T(8,128)S(1)}, f32[16,64]{1,0:T(8,128)}, u32[]{:S(2)}) copy-start(f32[16,64]{1,0:T(8,128)} %param.23) | copy-start | bytes 12292
  261.6 17.0 %copy-start.22 = (f32[16,64]{1,0:T(8,128)S(1)}, f32[16,64]{1,0:T(8,128)}, u32[]{:S(2)}) copy-start(f32[16,64]{1,0:T(8,128)} %param.24) | copy-start | bytes 12292
  261.7 16.9 %copy-start.23 = (f32[16,64]{1,0:T(8,128)S(1)}, f32[16,64]{1,0:T(8,128)}, u32[]{:S(2)}) copy-start(f32[16,64]{1,0:T(8,128)} %param.25) | copy-start | bytes 12292
  (10 other events, 19.2 us)
Sparse Core Ops, SparseCore 0:
  205.4 46.8 all-reduce.5
where the time goes:
time: 291 us; the launch traced here: 287 us
  local copies, waits for them, and re-layouts  91.2 us (31%)
  waiting for transfers between devices  89.3 us (31%)
  matrix products  40.9 us (14%)
  other arithmetic  25.4 us (9%)
  starting transfers between devices  15.6 us (5%)
  between operations  14.8 us (5%)
  blocking collectives  9.34 us (3%)
    psum x1, waiting for transfers between devices, shards(): param_grad = lax.psum(local_grad, 'dp')  46.4 us
    all_to_all x1, waiting for transfers between devices, shards(): lax.all_to_all(outgoing, 'expert', split_axis=0, concat_axis=1, tiled=True)  35.9 us
    gather x3, local copies, waits for them, and re-layouts, pick_rows(): return jnp.take(buffer, slot_index, axis=0, mode='fill', fill_value=0)  30.4 us
    unnamed x66, local copies, waits for them, and re-layouts  18.5 us
    scatter x1, other arithmetic, place_rows(): return blank.at[slot_index].set(rows, mode='drop')  13.5 us
    dot_general x4, matrix products, hidden_pass(): jnp.einsum('enr,erw->enw', current, matrix, preferred_element_type=jnp.fl...  13.4 us
    dot_general x4, matrix products, hidden_grads(): jnp.einsum('enr,enw->erw', activations[layer_index], pre_grad, preferred_...  12.7 us
    scatter x1, local copies, waits for them, and re-layouts, place_rows(): return blank.at[slot_index].set(rows, mode='drop')  11.4 us
  transfers between devices with their start and end apart: 4, of which 3 were waited for; matrix products, arithmetic and copies ran while one was open for 8% of the time, Pallas kernels for 0%

commit v1 on v0

--- a/solution.py
+++ b/solution.py
@@ -182,7 +182,11 @@
         code_back, "expert", split_axis=1, concat_axis=0, tiled=True
     ).reshape(slots_all, CODE_WIDTH)
     local_grad = assemble(weight_grads, bias_grads, hidden_grad, code_grad_head, bias_grad_head)
-    param_grad = lax.psum(local_grad, "dp")
+    param_grad = local_grad
+    for hop in (1, 2):
+        param_grad = param_grad + lax.ppermute(
+            param_grad, "dp", [(dev, dev ^ hop) for dev in range(4)]
+        )
     sample_code_grad = pick_rows(code_slot_grad, slot_index).reshape(ray_rows, SAMPLES, CODE_WIDTH)
     ray_code_grad = jnp.sum(sample_code_grad, axis=1)
     table_grad = lax.dot_general(

time: 291 us -> 259 us (0.89)
  waiting for transfers between devices: 89.3 us -> 75.2 us
  between operations: 14.8 us -> 1.51 us
  matrix products: 40.9 us -> 32.4 us
  other arithmetic: 25.4 us -> 29.5 us
    psum x1 -> x0, waiting for transfers between devices: 46.4 us -> none  [shards(): param_grad = lax.psum(local_grad, 'dp')]
    all_to_all x1, waiting for transfers between devices: 0.01 us -> 32.3 us  [shards(): lax.all_to_all(code_back, 'expert', split_axis=1, concat_axis=0, tiled=True)]
    dot_general x4, matrix products: 12.7 us -> 5.18 us  [hidden_grads(): jnp.einsum('enr,enw->erw', activations[layer_index], pre_grad, preferred_...]
    add x0 -> x1, other arithmetic: none -> 3.41 us  [shards(): param_grad + lax.ppermute(param_grad, 'dp', [(dev, dev ^ hop) for dev in...]
    unnamed x66 -> x60, local copies, waits for them, and re-layouts: 18.5 us -> 19.2 us
  transfers between devices with their start and end apart: 4 -> 5, of which waited for: 3 -> 3; matrix products, arithmetic and copies ran while one was open for 8% -> 14% of each run, Pallas kernels for 0% -> 0%
where the time goes in v1:
time: 259 us; the launch traced here: 254 us
  local copies, waits for them, and re-layouts  89.5 us (35%)
  waiting for transfers between devices  75.2 us (29%)
  matrix products  32.4 us (13%)
  other arithmetic  29.5 us (11%)
  starting transfers between devices  16.9 us (7%)
  blocking collectives  9.34 us (4%)
    all_to_all x1, waiting for transfers between devices, shards(): lax.all_to_all(outgoing, 'expert', split_axis=0, concat_axis=1, tiled=True)  35.9 us
    all_to_all x1, waiting for transfers between devices, shards(): lax.all_to_all(code_back, 'expert', split_axis=1, concat_axis=0, tiled=True)  32.3 us
    gather x3, local copies, waits for them, and re-layouts, pick_rows(): return jnp.take(buffer, slot_index, axis=0, mode='fill', fill_value=0)  30.6 us
    unnamed x60, local copies, waits for them, and re-layouts  19.2 us
    scatter x1, other arithmetic, place_rows(): return blank.at[slot_index].set(rows, mode='drop')  13.5 us
    dot_general x4, matrix products, hidden_pass(): jnp.einsum('enr,erw->enw', current, matrix, preferred_element_type=jnp.fl...  13.4 us
    scatter x1, local copies, waits for them, and re-layouts, place_rows(): return blank.at[slot_index].set(rows, mode='drop')  11.4 us
    all_to_all x1, blocking collectives, shards(): lax.all_to_all(cot_slots, 'expert', split_axis=0, concat_axis=1, tiled=True)  9.34 us
  transfers between devices with their start and end apart: 5, of which 3 were waited for; matrix products, arithmetic and copies ran while one was open for 14% of the time, Pallas kernels for 0%

profile of v1, /device:TPU:0, one launch (start us, length us, event | category | flops | bytes accessed | tf_op | source)
XLA Modules:
  0.0 254.4 jit_solution(17858865431749198511)
XLA Ops:
  6.9 13.5 %scatter_custom_fusion = bf16[6144,128]{1,0:T(8,128)(2,1)} fusion(s32[4096]{0:T(1024)S(1)} %bitcast.82, bf16[4096,64]{1,0:T(8,128)(2,1)} %bitcast.74, bf16[]{:T(256)} %constant.118, bf16[4096,64]{1,0:T(8,128)(2,1)S(1)} %bitcast.73, bf16[]{:T(256)} %constant.35.clone.1), kind=kCustom, calls=%fused_computation.37 | custom fusion | flops 2097152 | bytes 3145732 | tf_op jit(solution)/shard_map/scatter | solution.py:38
  20.4 7.6 %all-to-all-start = ((bf16[16,384,128]{2,1,0:T(8,128)(2,1)}), bf16[16,384,128]{2,1,0:T(8,128)(2,1)S(1)}, u32[]{:S(2)}, u32[]{:S(2)}) async-start(bf16[16,384,128]{2,1,0:T(8,128)(2,1)} %bitcast.70), calls=%async_computation | async-start | bytes 3145728 | tf_op jit(solution)/shard_map/all_to_all | solution.py:145
  29.1 35.9 %all-to-all-done = bf16[16,384,128]{2,1,0:T(8,128)(2,1)S(1)} async-done(((bf16[16,384,128]{2,1,0:T(8,128)(2,1)}), bf16[16,384,128]{2,1,0:T(8,128)(2,1)S(1)}, u32[]{:S(2)}, u32[]{:S(2)}) %all-to-all-start) | async-done | bytes 1572896 | tf_op jit(solution)/shard_map/all_to_all | solution.py:145
  66.9 4.1 %fusion.2 = (u8[3072,256]{1,0:T(8,128)(4,1)}, f32[2,3072,256]{2,1,0:T(8,128)S(1)}) fusion(f32[2,256]{1,0:T(2,128)S(1)} %bitcast.88, bf16[2,848,256]{2,1,0:T(8,128)(2,1)} %copy-done.8, bf16[2,3072,128]{1,2,0:T(8,128)(2,1)S(1)} %all_to_all.51), kind=kOutput, calls=%fused_computation.32 | convolution fusion | flops 209977344 | bytes 7931904 | tf_op jit(solution)/shard_map/enr,erw->enw/dot_general | solution.py:56
  71.0 3.1 %fusion.3 = (u8[3072,256]{1,0:T(8,128)(4,1)}, f32[2,3072,256]{2,1,0:T(8,128)S(1)}) fusion(f32[2,256]{1,0:T(2,128)S(1)} %get-tuple-element.38, bf16[2,848,256]{2,1,0:T(8,128)(2,1)S(1)} %copy-done.9, f32[2,3072,256]{2,1,0:T(8,128)S(1)} %get-tuple-element.28, f32[2,256]{1,0:T(2,128)S(1)} %bitcast.89), kind=kOutput, calls=%fused_computation.33 | convolution fusion | flops 818675712 | bytes 13635584 | tf_op jit(solution)/shard_map/enr,erw->enw/dot_general | solution.py:56
  74.1 3.1 %fusion.4 = (u8[3072,256]{1,0:T(8,128)(4,1)}, f32[2,3072,256]{2,1,0:T(8,128)S(1)}) fusion(f32[2,256]{1,0:T(2,128)S(1)} %get-tuple-element.37, bf16[2,848,256]{2,1,0:T(8,128)(2,1)S(1)} %copy-done.9, f32[2,3072,256]{2,1,0:T(8,128)S(1)} %get-tuple-element.26, f32[2,256]{1,0:T(2,128)S(1)} %get-tuple-element.38), kind=kOutput, calls=%fused_computation.34 | convolution fusion | flops 818675712 | bytes 13635584 | tf_op jit(solution)/shard_map/enr,erw->enw/dot_general | solution.py:56
  77.2 3.1 %fusion.5 = (u8[3072,256]{1,0:T(8,128)(4,1)}, f32[2,3072,256]{2,1,0:T(8,128)S(1)}) fusion(f32[2,256]{1,0:T(2,128)S(1)} %bitcast.85, bf16[2,848,256]{2,1,0:T(8,128)(2,1)S(1)} %copy-done.9, f32[2,3072,256]{2,1,0:T(8,128)S(1)} %get-tuple-element.24, f32[2,256]{1,0:T(2,128)S(1)} %get-tuple-element.37), kind=kOutput, calls=%fused_computation.35 | convolution fusion | flops 818675712 | bytes 13635584 | tf_op jit(solution)/shard_map/enr,erw->enw/dot_general | solution.py:56
  83.2 2.9 %copy.96 = f32[2,3072,4]{2,0,1:T(2,128)S(1)} copy(f32[2,3072,4]{1,2,0:T(4,128)S(1)} %fusion) | data formatting | bytes 196608 | tf_op jit(solution)/shard_map/add | solution.py:157
  86.1 5.6 %reshape.184 = f32[8,1,3072]{2,1,0:T(1,128)} reshape(f32[3072,2,4]{2,1,0:T(2,128)S(1)} %bitcast.67) | data formatting | bytes 196608
  91.7 4.2 %all-to-all-start.1 = ((f32[8,1,3072]{2,1,0:T(1,128)}), f32[8,1,3072]{2,1,0:T(1,128)S(1)}, u32[]{:S(2)}, u32[]{:S(2)}) async-start(f32[8,1,3072]{2,1,0:T(1,128)} %reshape.184), calls=%async_computation.1 | async-start | bytes 196608 | tf_op jit(solution)/shard_map/all_to_all | solution.py:158
  95.9 7.1 %all-to-all-done.1 = f32[8,1,3072]{2,1,0:T(1,128)S(1)} async-done(((f32[8,1,3072]{2,1,0:T(1,128)}), f32[8,1,3072]{2,1,0:T(1,128)S(1)}, u32[]{:S(2)}, u32[]{:S(2)}) %all-to-all-start.1) | async-done | bytes 98336 | tf_op jit(solution)/shard_map/all_to_all | solution.py:158
  104.4 6.6 %reshape.185 = f32[3072,2,4]{2,1,0:T(2,128)} reshape(f32[8,3072]{1,0:T(8,128)S(1)} %reduce.14) | data formatting | bytes 196608
  113.2 14.2 %gather_fusion = f32[4096,4]{1,0:T(8,128)} fusion(f32[6144,4]{1,0:T(8,128)S(1)} %bitcast.60, s32[4096]{0:T(1024)S(1)} %broadcast_clamp_fusion), kind=kCustom, calls=%fused_computation | custom fusion | bytes 147456 | tf_op jit(solution)/shard_map/jit(_take)/gather | solution.py:42
  131.9 11.4 %scatter_custom_fusion.1 = bf16[6144,4]{1,0:T(8,128)(2,1)S(1)} fusion(s32[4096]{0:T(1024)S(1)} %bitcast.84, bf16[4096,4]{1,0:T(8,128)(2,1)S(1)} %copy.113, bf16[]{:T(256)} %constant.35.clone.1), kind=kCustom, calls=%fused_computation.49 | custom fusion | bytes 49154 | tf_op jit(solution)/shard_map/scatter | solution.py:38
  144.0 9.3 %all_to_all.66 = bf16[16,384,4]{1,2,0:T(4,128)(2,1)S(1)} all-to-all(bf16[16,384,4]{1,2,0:T(4,128)(2,1)S(1)} %copy.114), channel_id=1, replica_groups=mesh['expert'=8,'dp'=4] {'expert'}, dimensions={0} | all-to-all | bytes 98304 | tf_op jit(solution)/shard_map/all_to_all | solution.py:169
  153.4 3.6 %fusion.16 = f32[2,4,256]{2,1,0:T(4,128)S(1)} fusion(bf16[2,3072,4]{1,2,0:T(4,128)(2,1)S(1)} %bitcast.75, f32[2,3072,256]{2,1,0:T(8,128)} %copy-done.3, f32[2,256]{1,0:T(2,128)S(1)} %bitcast.87), kind=kOutput, calls=%fused_computation.47 | convolution fusion | flops 17301504 | bytes 6350848 | tf_op jit(solution)/shard_map/enc,enw->ecw/dot_general | solution.py:172
  170.3 4.5 %concatenate.7 = f32[2,848,256]{2,1,0:T(8,128)} concatenate(f32[2,64,256]{2,1,0:T(8,128)S(1)} %fusion.24, f32[2,256,256]{2,1,0:T(8,128)S(1)} %fusion.10, f32[2,256,256]{2,1,0:T(8,128)S(1)} %fusion.12, f32[2,256,256]{2,1,0:T(8,128)S(1)} %fusion.14, f32[2,4,256]{2,1,0:T(4,128)S(1)} %fusion.16, f32[2,4,256]{2,1,0:T(4,128)S(1)} %pad.16, f32[2,1,256]{2,1,0:T(1,128)S(1)} %broadcast_in_dim.84, ...), dimensions={1} | concatenate | bytes 3473408 | tf_op jit(solution)/shard_map/concatenate | solution.py:96
  177.6 7.1 %copy.121 = f32[2,1536,128]{2,0,1:T(2,128)} copy(f32[2,1536,128]{2,1,0:T(8,128)} %reshape.134) | data formatting | bytes 3145728 | tf_op jit(solution)/shard_map/reshape | solution.py:180
  184.7 3.6 %all-to-all-start.3 = ((f32[2,1536,128]{2,0,1:T(2,128)}), f32[2,1536,128]{2,0,1:T(2,128)S(1)}, u32[]{:S(2)}, u32[]{:S(2)}) async-start(f32[2,1536,128]{2,0,1:T(2,128)} %copy.121), calls=%async_computation.3 | async-start | bytes 3145728 | tf_op jit(solution)/shard_map/all_to_all | solution.py:181
  188.3 3.4 %add.186 = f32[2,848,256]{2,1,0:T(8,128)} add(f32[2,848,256]{2,1,0:T(8,128)} %concatenate.7, f32[2,848,256]{2,1,0:T(8,128)} %collective-permute-done) | non-fusion elementwise | flops 434176 | bytes 5210112 | tf_op jit(solution)/shard_map/add | solution.py:187
  193.9 32.3 %all-to-all-done.3 = f32[2,1536,128]{2,0,1:T(2,128)S(1)} async-done(((f32[2,1536,128]{2,0,1:T(2,128)}), f32[2,1536,128]{2,0,1:T(2,128)S(1)}, u32[]{:S(2)}, u32[]{:S(2)}) %all-to-all-start.3) | async-done | bytes 1572896 | tf_op jit(solution)/shard_map/all_to_all | solution.py:181
  230.0 14.2 %gather_fusion.1 = f32[4096,64]{1,0:T(8,128)} fusion(f32[6144,64]{1,0:T(8,128)S(1)} %reshape.135, s32[4096]{0:T(1024)S(1)} %broadcast_clamp_fusion), kind=kCustom, calls=%fused_computation.1 | custom fusion | bytes 2113536 | tf_op jit(solution)/shard_map/jit(_take)/gather | solution.py:42
  244.2 3.0 %select_reduce_fusion = f32[128,64]{1,0:T(8,128)S(1)} fusion(pred[128,32]{1,0:T(8,128)(4,1)S(1)} %copy.119, f32[4096,64]{1,0:T(8,128)} %gather_fusion.1), kind=kLoop, calls=%fused_computation.28 | loop fusion | flops 516096 | bytes 1085440 | tf_op jit(solution)/shard_map/reduce_sum | solution.py:191
  248.1 6.1 %divide_subtract_fusion = (f32[2,848,256]{2,1,0:T(8,128)}, f32[2,848,256]{2,1,0:T(8,128)}, f32[2,848,256]{2,1,0:T(8,128)}) fusion(f32[2,848,256]{2,1,0:T(8,128)S(1)} %copy-done.5, f32[2,848,256]{2,1,0:T(8,128)} %add.186, f32[2,848,256]{2,1,0:T(8,128)} %collective-permute-done.1, f32[2,848,256]{2,1,0:T(8,128)} %param.21, f32[2,848,256]{2,1,0:T(8,128)} %param.22), kind=kLoop, calls=%fused_computation.30 | loop fusion | flops 5644288 | bytes 13893632 | tf_op jit(solution)/shard_map/sub | solution.py:23
  (140 shorter events, 43.6 us)
Async XLA Ops:
  6.9 21.2 %copy-start.4 = (f32[2,848,256]{2,1,0:T(8,128)S(1)}, f32[2,848,256]{2,1,0:T(8,128)}, u32[]{:S(2)}) copy-start(f32[2,848,256]{2,1,0:T(8,128)} %param.20) | copy-start | bytes 5210116
  20.4 44.6 %all-to-all-start = ((bf16[16,384,128]{2,1,0:T(8,128)(2,1)}), bf16[16,384,128]{2,1,0:T(8,128)(2,1)S(1)}, u32[]{:S(2)}, u32[]{:S(2)}) async-start(bf16[16,384,128]{2,1,0:T(8,128)(2,1)} %bitcast.70), calls=%async_computation | async-start | bytes 3145728 | tf_op jit(solution)/shard_map/all_to_all | solution.py:145
  66.9 16.1 %copy-start.6 = (bf16[2,3072,128]{1,2,0:T(8,128)(2,1)}, bf16[2,3072,128]{1,2,0:T(8,128)(2,1)S(1)}, u32[]{:S(2)}) copy-start(bf16[2,3072,128]{1,2,0:T(8,128)(2,1)S(1)} %all_to_all.51) | copy-start | bytes 4718596
  66.9 4.1 %copy-start.9 = (bf16[2,848,256]{2,1,0:T(8,128)(2,1)S(1)}, bf16[2,848,256]{2,1,0:T(8,128)(2,1)}, u32[]{:S(2)}) copy-start(bf16[2,848,256]{2,1,0:T(8,128)(2,1)} %copy-done.8) | copy-start | bytes 2605060
  71.0 3.1 %copy-start = (f32[2,3072,256]{2,1,0:T(8,128)}, f32[2,3072,256]{2,1,0:T(8,128)S(1)}, u32[]{:S(2)}) copy-start(f32[2,3072,256]{2,1,0:T(8,128)S(1)} %get-tuple-element.28) | copy-start | bytes 18874372
  74.1 3.1 %copy-start.1 = (f32[2,3072,256]{2,1,0:T(8,128)}, f32[2,3072,256]{2,1,0:T(8,128)S(1)}, u32[]{:S(2)}) copy-start(f32[2,3072,256]{2,1,0:T(8,128)S(1)} %get-tuple-element.26) | copy-start | bytes 18874372
  77.2 3.1 %copy-start.2 = (f32[2,3072,256]{2,1,0:T(8,128)}, f32[2,3072,256]{2,1,0:T(8,128)S(1)}, u32[]{:S(2)}) copy-start(f32[2,3072,256]{2,1,0:T(8,128)S(1)} %get-tuple-element.24) | copy-start | bytes 18874372
  80.4 2.6 %copy-start.3 = (f32[2,3072,256]{2,1,0:T(8,128)}, f32[2,3072,256]{2,1,0:T(8,128)S(1)}, u32[]{:S(2)}) copy-start(f32[2,3072,256]{2,1,0:T(8,128)S(1)} %get-tuple-element.22) | copy-start | bytes 18874372
  91.7 11.3 %all-to-all-start.1 = ((f32[8,1,3072]{2,1,0:T(1,128)}), f32[8,1,3072]{2,1,0:T(1,128)S(1)}, u32[]{:S(2)}, u32[]{:S(2)}) async-start(f32[8,1,3072]{2,1,0:T(1,128)} %reshape.184), calls=%async_computation.1 | async-start | bytes 196608 | tf_op jit(solution)/shard_map/all_to_all | solution.py:158
  113.2 16.7 %copy-start.15 = (f32[128,32]{0,1:T(8,128)S(1)}, f32[128,32]{0,1:T(8,128)}, u32[]{:S(2)}) copy-start(f32[128,32]{0,1:T(8,128)} %param.14) | copy-start | bytes 49156
  113.2 16.7 %copy-start.19 = (s32[128]{0:T(128)S(1)}, s32[128]{0:T(128)}, u32[]{:S(2)}) copy-start(s32[128]{0:T(128)} %param.16) | copy-start | bytes 1540
  127.5 2.9 %copy-start.20 = (f32[3,128]{1,0:T(4,128)S(1)}, f32[3,128]{1,0:T(4,128)}, u32[]{:S(2)}) copy-start(f32[3,128]{1,0:T(4,128)} %param.15) | copy-start | bytes 4612
  153.4 3.6 %copy-start.7 = (bf16[2,3072,128]{1,2,0:T(8,128)(2,1)S(1)}, bf16[2,3072,128]{1,2,0:T(8,128)(2,1)}, u32[]{:S(2)}) copy-start(bf16[2,3072,128]{1,2,0:T(8,128)(2,1)} %copy-done.6) | copy-start | bytes 4718596
  153.4 4.0 %copy-start.10 = (bf16[2,848,256]{2,1,0:T(8,128)(2,1)S(1)}, bf16[2,848,256]{2,1,0:T(8,128)(2,1)}, u32[]{:S(2)}) copy-start(bf16[2,848,256]{2,1,0:T(8,128)(2,1)} %copy-done.8) | copy-start | bytes 2605060
  153.4 4.0 %copy-start.14 = (u8[3072,256]{1,0:T(8,128)(4,1)S(1)}, u8[3072,256]{1,0:T(8,128)(4,1)}, u32[]{:S(2)}) copy-start(u8[3072,256]{1,0:T(8,128)(4,1)} %get-tuple-element.21) | copy-start | bytes 2359300
  160.0 2.9 %slice-start.2 = ((s8[6291456]{0:T(1024)(128)(4,1)}), s8[4194304]{0:T(1024)(128)(4,1)S(1)}, s32[]{:S(2)}) async-start(s8[6291456]{0:T(1024)(128)(4,1)} %bitcast.63), calls=%async_computation.6 | async-start | bytes 8388608
  163.3 2.9 %slice-start = ((s8[6291456]{0:T(1024)(128)(4,1)}), s8[4194304]{0:T(1024)(128)(4,1)S(1)}, s32[]{:S(2)}) async-start(s8[6291456]{0:T(1024)(128)(4,1)} %bitcast.61), calls=%async_computation.4 | async-start | bytes 8388608
  174.7 13.6 %collective-permute-start = (f32[2,848,256]{2,1,0:T(8,128)}, f32[2,848,256]{2,1,0:T(8,128)}, u32[]{:S(2)}, u32[]{:S(2)}) collective-permute-start(f32[2,848,256]{2,1,0:T(8,128)} %concatenate.7), channel_id=1, source_target_pairs={{0,1},{1,0},{2,3},{3,2},{4,5},{5,4},{6,7},{7,6},{8,9},{9,8},{10,11... | collective-permute-start | bytes 5210120 | tf_op jit(solution)/shard_map/ppermute | solution.py:187
  184.7 41.5 %all-to-all-start.3 = ((f32[2,1536,128]{2,0,1:T(2,128)}), f32[2,1536,128]{2,0,1:T(2,128)S(1)}, u32[]{:S(2)}, u32[]{:S(2)}) async-start(f32[2,1536,128]{2,0,1:T(2,128)} %copy.121), calls=%async_computation.3 | async-start | bytes 3145728 | tf_op jit(solution)/shard_map/all_to_all | solution.py:181
  191.7 56.3 %collective-permute-start.1 = (f32[2,848,256]{2,1,0:T(8,128)}, f32[2,848,256]{2,1,0:T(8,128)}, u32[]{:S(2)}, u32[]{:S(2)}) collective-permute-start(f32[2,848,256]{2,1,0:T(8,128)} %add.186), channel_id=1, source_target_pairs={{0,2},{1,3},{2,0},{3,1},{4,6},{5,7},{6,4},{7,5},{8,10},{9,11},{10,... | collective-permute-start | bytes 5210120 | tf_op jit(solution)/shard_map/ppermute | solution.py:187
  230.0 17.2 %copy-start.16 = (f32[16,64]{1,0:T(8,128)S(1)}, f32[16,64]{1,0:T(8,128)}, u32[]{:S(2)}) copy-start(f32[16,64]{1,0:T(8,128)} %param.23) | copy-start | bytes 12292
  230.0 17.2 %copy-start.17 = (f32[16,64]{1,0:T(8,128)S(1)}, f32[16,64]{1,0:T(8,128)}, u32[]{:S(2)}) copy-start(f32[16,64]{1,0:T(8,128)} %param.24) | copy-start | bytes 12292
  230.0 17.2 %copy-start.18 = (f32[16,64]{1,0:T(8,128)S(1)}, f32[16,64]{1,0:T(8,128)}, u32[]{:S(2)}) copy-start(f32[16,64]{1,0:T(8,128)} %param.25) | copy-start | bytes 12292
  244.1 3.9 %copy-start.5 = (f32[2,848,256]{2,1,0:T(8,128)S(1)}, f32[2,848,256]{2,1,0:T(8,128)}, u32[]{:S(2)}) copy-start(f32[2,848,256]{2,1,0:T(8,128)} %param.20) | copy-start | bytes 5210116
  (8 other events, 13.9 us)
